TPU v7x, 512 devices: a whole 4x4x16 slice. The times are simulated.
512 devices in a mesh: ta: 8 (over y, z_hi), ha: 4 (over x), wa: 16 (over z_lo, core).
Axes of the slice: x: 4, y: 4, z: 16 (z_hi: 2, z_lo: 8; z = z_hi * 8 + z_lo), core: 2. Of those that a mesh axis runs over, the one named last changes fastest.
Arguments:
- features: bfloat16 [16, 64, 256, 256], P('ta', 'ha', 'wa'), may hold values from -6 to 6
- conv_weight: bfloat16 [6912, 256], P('wa'), may hold values from -0.078125 to 0.078125
- down_weight: bfloat16 [2, 2, 256, 256], replicated, may hold values from -0.1875 to 0.1875
- grad_out: bfloat16 [16, 32, 128, 256], P('ta', 'ha', 'wa'), may hold values from -6 to 6
- crop_grad: bfloat16 [32768, 8, 8, 256], P(('ta', 'ha', 'wa')), may hold values from -6 to 6
- crop_owner: int32 [32768, 1], P(('ta', 'ha', 'wa')), may hold values from 0 to 63; in each aligned block of 64 rows (0 to 63, 64 to 127, ...) at most 2 rows name the same one
- crop_frame: int32 [32768], P(('ta', 'ha', 'wa')), may hold values from 0 to 1
- crop_row: int32 [32768], P(('ta', 'ha', 'wa')), may hold values from 0 to 8
- crop_col: int32 [32768], P(('ta', 'ha', 'wa')), may hold values from 0 to 8
- crop_valid: int32 [32768], P(('ta', 'ha', 'wa')), may hold values 0 or 1
Outputs:
- reduced: bfloat16 [16, 32, 128, 256], P('ta', 'ha', 'wa')
- grad_in: bfloat16 [16, 64, 256, 256], P('ta', 'ha', 'wa')
Inputs may be any that keep to these rules, and one draw needn't show every extreme that they name: `crop_owner`: among one device's 64 crops at most 2 name the same owner, a bound that some block reaches; the owner is the tile of the same time slab whose height index is the value divided by the number of width tiles and whose width index is the remainder. `crop_frame`: frame of the crop within the time slab of the device that holds it. `crop_valid`: padding crops carry gradients that are ignored.
All inputs are finite; a program needn't handle non-finite values. No bound on the sum of `crop_valid` on one device may be relied on, other than what follows from the above.
Results may differ from a plain program's by a relative error of at most 0.0049.
Values may be sent and summed in bfloat16 or wider, within the bound.
A program may use at most 64 MiB of HBM per device.

v0:
```python
import jax
import jax.numpy as jnp
from jax import lax
from jax.sharding import PartitionSpec as P

CH = 8
CW = 8
CAP = 2


def extended(block, sides, width):
    for axis, dim in sides:
        count = lax.axis_size(axis)
        forward = [(i, i + 1) for i in range(count - 1)]
        backward = [(target, source) for source, target in forward]
        low = lax.ppermute(
            lax.slice_in_dim(block, block.shape[dim] - width, None, axis=dim), axis, forward
        )
        high = lax.ppermute(lax.slice_in_dim(block, 0, width, axis=dim), axis, backward)
        block = jnp.concatenate([low, block, high], axis=dim)
    return block


def from_behind(value, axis, steps):
    count = lax.axis_size(axis)
    first, last = (max(0, -steps), min(count, count - steps))
    return lax.ppermute(value, axis, [(source, source + steps) for source in range(first, last)])


def convolve(padded, kernel_taps, frames, rows, cols):
    width = kernel_taps.shape[-1]
    summed = jnp.zeros((frames * rows * cols, width), jnp.float32)
    for frame_off in range(3):
        windows = []
        for row_off in range(3):
            for col_off in range(3):
                windows.append(
                    padded[
                        frame_off : frame_off + frames,
                        row_off : row_off + rows,
                        col_off : col_off + cols,
                        :,
                    ]
                )
        stacked = jnp.concatenate(windows, -1).reshape(frames * rows * cols, 9 * width)
        tap_block = kernel_taps[frame_off * 9 : (frame_off + 1) * 9].reshape(9 * width, width)
        summed = summed + jnp.dot(stacked, tap_block, preferred_element_type=jnp.float32)
    return summed.reshape(frames, rows, cols, width)


def widen(block):
    return extended(block, (("ha", 1), ("wa", 2)), 1)


def per_device(
    features,
    conv_weight,
    down_weight,
    grad_out,
    crop_grad,
    crop_owner,
    crop_frame,
    crop_row,
    crop_col,
    crop_valid,
):
    frames, rows, cols, width = features.shape
    height_tiles = lax.axis_size("ha")
    width_tiles = lax.axis_size("wa")
    owners_all = height_tiles * width_tiles
    slots_all = owners_all * CAP
    count = crop_owner.shape[0]
    owner_id = crop_owner[:, 0]
    onehot = (owner_id[:, None] == jnp.arange(owners_all, dtype=jnp.int32)[None, :]).astype(
        jnp.int32
    )
    earlier = jnp.cumsum(onehot, 0) - onehot
    slot_rank = jnp.sum(earlier * onehot, 1)
    target = owner_id * CAP + slot_rank
    placing = target[:, None] == jnp.arange(slots_all, dtype=jnp.int32)[None, :]
    weighted = crop_grad * crop_valid.astype(jnp.bfloat16)[:, None, None, None]
    packed = jnp.dot(
        placing.astype(jnp.bfloat16).T,
        weighted.reshape(count, -1),
        preferred_element_type=jnp.float32,
    ).astype(jnp.bfloat16)
    place_meta = jnp.stack([crop_frame, crop_row, crop_col], 1)
    meta_sent = jnp.sum(placing.astype(jnp.int32)[:, :, None] * place_meta[:, None, :], 0)
    received, got_meta = (
        lax.all_to_all(packed, ("ha", "wa"), split_axis=0, concat_axis=0, tiled=True),
        lax.all_to_all(meta_sent, ("ha", "wa"), split_axis=0, concat_axis=0, tiled=True),
    )
    row_steps = jnp.arange(CH, dtype=jnp.int32)
    col_steps = jnp.arange(CW, dtype=jnp.int32)
    cell_index = (
        (got_meta[:, 0, None, None] * rows + got_meta[:, 1, None, None] + row_steps[None, :, None])
        * cols
        + got_meta[:, 2, None, None]
        + col_steps[None, None, :]
    )
    crop_terms = (
        jnp.zeros((frames * rows * cols, width), jnp.float32)
        .at[cell_index.reshape(-1)]
        .add(received.reshape(-1, width).astype(jnp.float32))
    )
    gathered = lax.all_gather(conv_weight, "wa", axis=0, tiled=True)
    kernel_taps = gathered.reshape(27, width, width)
    past = from_behind(features, "ta", 1)
    padded = widen(jnp.concatenate([past, features], 0))
    preact = convolve(padded, kernel_taps, frames, rows, cols)
    sigmoid_h = jax.nn.sigmoid(preact)
    section_out = (features.astype(jnp.float32) + preact * sigmoid_h).astype(jnp.bfloat16)
    down_mat = down_weight.reshape(4 * width, width)
    pooled = (
        section_out.reshape(frames, rows // 2, 2, cols // 2, 2, width)
        .transpose(0, 1, 3, 2, 4, 5)
        .reshape(-1, 4 * width)
    )
    reduced = (
        jnp.dot(pooled, down_mat, preferred_element_type=jnp.float32)
        .astype(jnp.bfloat16)
        .reshape(frames, rows // 2, cols // 2, width)
    )
    spread = jnp.dot(grad_out.reshape(-1, width), down_mat.T, preferred_element_type=jnp.float32)
    spread = (
        spread.reshape(frames, rows // 2, cols // 2, 2, 2, width)
        .transpose(0, 1, 3, 2, 4, 5)
        .reshape(frames, rows, cols, width)
    )
    grad_pre = (spread * sigmoid_h * (1.0 + preact * (1.0 - sigmoid_h))).astype(jnp.bfloat16)
    flipped = jnp.transpose(kernel_taps[::-1], (0, 2, 1))
    future = from_behind(grad_pre, "ta", -1)
    back_pad = widen(jnp.concatenate([grad_pre, future], 0))
    through = convolve(back_pad, flipped, frames, rows, cols)
    grad_in = (spread + through + crop_terms.reshape(frames, rows, cols, width)).astype(
        jnp.bfloat16
    )
    return (reduced, grad_in)


def solution(mesh):
    in_specs = (
        P("ta", "ha", "wa", None),
        P("wa", None),
        P(),
        P("ta", "ha", "wa", None),
        P(("ta", "ha", "wa"), None, None, None),
        P(("ta", "ha", "wa"), None),
        P(("ta", "ha", "wa")),
        P(("ta", "ha", "wa")),
        P(("ta", "ha", "wa")),
        P(("ta", "ha", "wa")),
    )
    out_specs = (P("ta", "ha", "wa", None), P("ta", "ha", "wa", None))
    return jax.shard_map(
        per_device, mesh=mesh, in_specs=in_specs, out_specs=out_specs, check_vma=False
    )
```

profile of v0, /device:TPU:27, one launch (start us, length us, event | category | flops | bytes accessed | tf_op | source)
XLA Modules:
  0.0 448.2 jit_solution(8883349491360563896)
XLA Ops:
  11.2 16.4 %all-to-all-start = ((s32[64,2,3]{2,1,0:T(2,128)}), s32[64,2,3]{2,1,0:T(2,128)S(1)}, u32[]{:S(2)}, u32[]{:S(2)}) async-start(s32[64,2,3]{2,1,0:T(2,128)} %bitcast.28), calls=%async_computation | async-start | bytes 131072 | tf_op jit(solution)/shard_map/all_to_all | solution.py:91
  31.4 3.3 convolution_convert_fusion
  34.7 7.7 %all_to_all.17 = bf16[64,2,16384]{2,1,0:T(2,128)(2,1)} reshape(bf16[128,16384]{1,0:T(8,128)(2,1)} %convolution_convert_fusion) | data formatting | bytes 8388608 | tf_op jit(solution)/shard_map/all_to_all | solution.py:90
  42.4 13.4 %all-to-all-start.1 = ((bf16[64,2,16384]{2,1,0:T(2,128)(2,1)}), bf16[64,2,16384]{2,1,0:T(2,128)(2,1)}, u32[]{:S(2)}, u32[]{:S(2)}) async-start(bf16[64,2,16384]{2,1,0:T(2,128)(2,1)} %all_to_all.17), calls=%async_computation.1 | async-start | bytes 8388608 | tf_op jit(solution)/shard_map/all_to_all | solution.py:90
  56.5 7.9 %collective-permute-start = (bf16[2,16,16,256]{3,2,1,0:T(8,128)(2,1)S(1)}, bf16[2,16,16,256]{3,2,1,0:T(8,128)(2,1)S(1)}, u32[]{:S(2)}, u32[]{:S(2)}) collective-permute-start(bf16[2,16,16,256]{3,2,1,0:T(8,128)(2,1)S(1)} %copy-done.3), channel_id=1, source_target_pairs={{0,64},{64,128},{128,192},{192,256},{256,320},{320,384},{384,448},... | collective-permute-start | bytes 786440 | tf_op jit(solution)/shard_map/ppermute | solution.py:27
  65.7 109.0 %collective-permute-done = bf16[2,16,16,256]{3,2,1,0:T(8,128)(2,1)S(1)} collective-permute-done((bf16[2,16,16,256]{3,2,1,0:T(8,128)(2,1)S(1)}, bf16[2,16,16,256]{3,2,1,0:T(8,128)(2,1)S(1)}, u32[]{:S(2)}, u32[]{:S(2)}) %collective-permute-start) | collective-permute-done | bytes 262176 | tf_op jit(solution)/shard_map/ppermute | solution.py:27
  174.7 3.2 collective-permute-start.1
  177.9 2.1 collective-permute-start.2
  180.5 2.5 collective-permute-done.2
  183.2 1.9 collective-permute-start.3
  185.1 3.1 collective-permute-start.4
  188.3 4.0 collective-permute-done.4
  203.2 43.4 %all-gather.2.cloned.1.call-done = bf16[6912,256]{1,0:T(8,128)(2,1)} async-done(((bf16[432,256]{1,0:T(8,128)(2,1)}), bf16[6912,256]{1,0:T(8,128)(2,1)}) %all-gather.2.cloned.1.call-update) | async-done | bytes 3538960 | tf_op jit(solution)/shard_map/all_gather | solution.py:106
  246.5 2.9 fusion.2
  249.6 2.4 convolution_add_fusion.3
  252.0 2.4 convolution_add_fusion.2
  254.8 13.7 %collective-permute-start.5 = (bf16[2,16,16,256]{3,2,1,0:T(8,128)(2,1)S(1)}, bf16[2,16,16,256]{3,2,1,0:T(8,128)(2,1)S(1)}, u32[]{:S(2)}, u32[]{:S(2)}) collective-permute-start(bf16[2,16,16,256]{3,2,1,0:T(8,128)(2,1)S(1)} %get-tuple-element.75), channel_id=1, source_target_pairs={{64,0},{128,64},{192,128},{256,192},{320,256},{384,320},{448,384},... | collective-permute-start | bytes 786440 | tf_op jit(solution)/shard_map/ppermute | solution.py:27
  269.0 2.4 reverse_bitcast_fusion
  273.1 4.5 %collective-permute-start.6 = (bf16[4,1,16,256]{3,2,1,0:T(8,128)(2,1)S(1)}, bf16[4,1,16,256]{3,2,1,0:T(8,128)(2,1)S(1)}, u32[]{:S(2)}, u32[]{:S(2)}) collective-permute-start(bf16[4,1,16,256]{3,2,1,0:T(8,128)(2,1)S(1)} %get-tuple-element.73), channel_id=1, source_target_pairs={{0,16},{16,32},{32,48},{1,17},{17,33},{33,49},{2,18},{18,34},{34,5... | collective-permute-start | bytes 98312 | tf_op jit(solution)/shard_map/ppermute | solution.py:16
  280.5 2.4 copy.76
  286.1 90.1 %collective-permute-start.8 = (bf16[4,18,1,256]{3,2,1,0:T(2,128)(2,1)S(1)}, bf16[4,18,1,256]{3,2,1,0:T(2,128)(2,1)S(1)}, u32[]{:S(2)}, u32[]{:S(2)}) collective-permute-start(bf16[4,18,1,256]{3,2,1,0:T(2,128)(2,1)S(1)} %get-tuple-element.54), channel_id=1, source_target_pairs={{0,1},{1,2},{2,3},{3,4},{4,5},{5,6},{6,7},{7,8},{8,9},{9,10},{10,1... | collective-permute-start | bytes 110600 | tf_op jit(solution)/shard_map/ppermute | solution.py:16
  378.3 3.6 collective-permute-done.9
  386.8 8.2 %reshape.228 = f32[8192,256]{1,0:T(8,128)} reshape(bf16[64,2,16384]{2,1,0:T(2,128)(2,1)} %all-to-all-done.1) | data formatting | bytes 12582912 | tf_op jit(solution)/shard_map/convert_element_type | solution.py:104
  395.0 44.7 %scatter_custom_fusion = f32[512,256]{1,0:T(8,128)S(1)} fusion(s32[8192]{0:T(1024)S(1)} %bitcast.83, f32[8192,256]{1,0:T(8,128)} %reshape.228, f32[]{:T(128)} %constant.7.clone.1), kind=kCustom, calls=%fused_computation.96 | custom fusion | flops 2097152 | bytes 524800 | tf_op jit(solution)/shard_map/scatter-add | solution.py:104
  (88 shorter events, 38.3 us)
Async XLA Ops:
  7.2 57.3 %copy-start = (bf16[2,2,256,256]{3,2,1,0:T(8,128)(2,1)S(1)}, bf16[2,2,256,256]{3,2,1,0:T(8,128)(2,1)}, u32[]{:S(2)}) copy-start(bf16[2,2,256,256]{3,2,1,0:T(8,128)(2,1)} %param.12) | copy-start | bytes 1572868
  11.2 31.2 %all-to-all-start = ((s32[64,2,3]{2,1,0:T(2,128)}), s32[64,2,3]{2,1,0:T(2,128)S(1)}, u32[]{:S(2)}, u32[]{:S(2)}) async-start(s32[64,2,3]{2,1,0:T(2,128)} %bitcast.28), calls=%async_computation | async-start | bytes 131072 | tf_op jit(solution)/shard_map/all_to_all | solution.py:91
  42.4 14.1 %copy-start.3 = (bf16[2,16,16,256]{3,2,1,0:T(8,128)(2,1)S(1)}, bf16[2,16,16,256]{3,2,1,0:T(8,128)(2,1)}, u32[]{:S(2)}) copy-start(bf16[2,16,16,256]{3,2,1,0:T(8,128)(2,1)} %param.10) | copy-start | bytes 786436
  42.4 22.1 %copy-start.5 = (bf16[2,8,8,256]{3,2,1,0:T(8,128)(2,1)S(1)}, bf16[2,8,8,256]{3,2,1,0:T(8,128)(2,1)}, u32[]{:S(2)}) copy-start(bf16[2,8,8,256]{3,2,1,0:T(8,128)(2,1)} %param.13) | copy-start | bytes 196612
  42.4 344.4 %all-to-all-start.1 = ((bf16[64,2,16384]{2,1,0:T(2,128)(2,1)}), bf16[64,2,16384]{2,1,0:T(2,128)(2,1)}, u32[]{:S(2)}, u32[]{:S(2)}) async-start(bf16[64,2,16384]{2,1,0:T(2,128)(2,1)} %all_to_all.17), calls=%async_computation.1 | async-start | bytes 8388608 | tf_op jit(solution)/shard_map/all_to_all | solution.py:90
  55.8 190.8 %all-gather.2.cloned.1.call-start = ((), (), s32[]{:S(2)}) async-start(), calls=%async_computation.2 | async-start | bytes 3760128 | tf_op jit(solution)/shard_map/all_gather | solution.py:106
  56.5 118.1 %collective-permute-start = (bf16[2,16,16,256]{3,2,1,0:T(8,128)(2,1)S(1)}, bf16[2,16,16,256]{3,2,1,0:T(8,128)(2,1)S(1)}, u32[]{:S(2)}, u32[]{:S(2)}) collective-permute-start(bf16[2,16,16,256]{3,2,1,0:T(8,128)(2,1)S(1)} %copy-done.3), channel_id=1, source_target_pairs={{0,64},{64,128},{128,192},{192,256},{256,320},{320,384},{384,448},... | collective-permute-start | bytes 786440 | tf_op jit(solution)/shard_map/ppermute | solution.py:27
  174.7 5.8 %collective-permute-start.1 = (bf16[4,1,16,256]{3,2,1,0:T(8,128)(2,1)S(1)}, bf16[4,1,16,256]{3,2,1,0:T(8,128)(2,1)S(1)}, u32[]{:S(2)}, u32[]{:S(2)}) collective-permute-start(bf16[4,1,16,256]{3,2,1,0:T(8,128)(2,1)S(1)} %get-tuple-element.77), channel_id=1, source_target_pairs={{0,16},{16,32},{32,48},{1,17},{17,33},{33,49},{2,18},{18,34},{34,5... | collective-permute-start | bytes 98312 | tf_op jit(solution)/shard_map/ppermute | solution.py:16
  177.9 5.2 %collective-permute-start.2 = (bf16[4,1,16,256]{3,2,1,0:T(8,128)(2,1)S(1)}, bf16[4,1,16,256]{3,2,1,0:T(8,128)(2,1)S(1)}, u32[]{:S(2)}, u32[]{:S(2)}) collective-permute-start(bf16[4,1,16,256]{3,2,1,0:T(8,128)(2,1)S(1)} %get-tuple-element.78), channel_id=1, source_target_pairs={{16,0},{32,16},{48,32},{17,1},{33,17},{49,33},{18,2},{34,18},{50,3... | collective-permute-start | bytes 98312 | tf_op jit(solution)/shard_map/ppermute | solution.py:19
  183.2 5.1 %collective-permute-start.3 = (bf16[4,18,1,256]{3,2,1,0:T(2,128)(2,1)S(1)}, bf16[4,18,1,256]{3,2,1,0:T(2,128)(2,1)S(1)}, u32[]{:S(2)}, u32[]{:S(2)}) collective-permute-start(bf16[4,18,1,256]{3,2,1,0:T(2,128)(2,1)S(1)} %get-tuple-element.58), channel_id=1, source_target_pairs={{0,1},{1,2},{2,3},{3,4},{4,5},{5,6},{6,7},{7,8},{8,9},{9,10},{10,1... | collective-permute-start | bytes 110600 | tf_op jit(solution)/shard_map/ppermute | solution.py:16
  185.1 7.2 %collective-permute-start.4 = (bf16[4,18,1,256]{3,2,1,0:T(2,128)(2,1)S(1)}, bf16[4,18,1,256]{3,2,1,0:T(2,128)(2,1)S(1)}, u32[]{:S(2)}, u32[]{:S(2)}) collective-permute-start(bf16[4,18,1,256]{3,2,1,0:T(2,128)(2,1)S(1)} %get-tuple-element.57), channel_id=1, source_target_pairs={{1,0},{2,1},{3,2},{4,3},{5,4},{6,5},{7,6},{8,7},{9,8},{10,9},{11,1... | collective-permute-start | bytes 110600 | tf_op jit(solution)/shard_map/ppermute | solution.py:19
  246.5 3.1 copy-start.2
  254.8 18.3 %collective-permute-start.5 = (bf16[2,16,16,256]{3,2,1,0:T(8,128)(2,1)S(1)}, bf16[2,16,16,256]{3,2,1,0:T(8,128)(2,1)S(1)}, u32[]{:S(2)}, u32[]{:S(2)}) collective-permute-start(bf16[2,16,16,256]{3,2,1,0:T(8,128)(2,1)S(1)} %get-tuple-element.75), channel_id=1, source_target_pairs={{64,0},{128,64},{192,128},{256,192},{320,256},{384,320},{448,384},... | collective-permute-start | bytes 786440 | tf_op jit(solution)/shard_map/ppermute | solution.py:27
  273.1 12.8 %collective-permute-start.6 = (bf16[4,1,16,256]{3,2,1,0:T(8,128)(2,1)S(1)}, bf16[4,1,16,256]{3,2,1,0:T(8,128)(2,1)S(1)}, u32[]{:S(2)}, u32[]{:S(2)}) collective-permute-start(bf16[4,1,16,256]{3,2,1,0:T(8,128)(2,1)S(1)} %get-tuple-element.73), channel_id=1, source_target_pairs={{0,16},{16,32},{32,48},{1,17},{17,33},{33,49},{2,18},{18,34},{34,5... | collective-permute-start | bytes 98312 | tf_op jit(solution)/shard_map/ppermute | solution.py:16
  277.7 8.3 %collective-permute-start.7 = (bf16[4,1,16,256]{3,2,1,0:T(8,128)(2,1)S(1)}, bf16[4,1,16,256]{3,2,1,0:T(8,128)(2,1)S(1)}, u32[]{:S(2)}, u32[]{:S(2)}) collective-permute-start(bf16[4,1,16,256]{3,2,1,0:T(8,128)(2,1)S(1)} %get-tuple-element.74), channel_id=1, source_target_pairs={{16,0},{32,16},{48,32},{17,1},{33,17},{49,33},{18,2},{34,18},{50,3... | collective-permute-start | bytes 98312 | tf_op jit(solution)/shard_map/ppermute | solution.py:19
  286.1 92.1 %collective-permute-start.8 = (bf16[4,18,1,256]{3,2,1,0:T(2,128)(2,1)S(1)}, bf16[4,18,1,256]{3,2,1,0:T(2,128)(2,1)S(1)}, u32[]{:S(2)}, u32[]{:S(2)}) collective-permute-start(bf16[4,18,1,256]{3,2,1,0:T(2,128)(2,1)S(1)} %get-tuple-element.54), channel_id=1, source_target_pairs={{0,1},{1,2},{2,3},{3,4},{4,5},{5,6},{6,7},{7,8},{8,9},{9,10},{10,1... | collective-permute-start | bytes 110600 | tf_op jit(solution)/shard_map/ppermute | solution.py:16
  376.2 5.7 %collective-permute-start.9 = (bf16[4,18,1,256]{3,2,1,0:T(2,128)(2,1)S(1)}, bf16[4,18,1,256]{3,2,1,0:T(2,128)(2,1)S(1)}, u32[]{:S(2)}, u32[]{:S(2)}) collective-permute-start(bf16[4,18,1,256]{3,2,1,0:T(2,128)(2,1)S(1)} %get-tuple-element.53), channel_id=1, source_target_pairs={{1,0},{2,1},{3,2},{4,3},{5,4},{6,5},{7,6},{8,7},{9,8},{10,9},{11,1... | collective-permute-start | bytes 110600 | tf_op jit(solution)/shard_map/ppermute | solution.py:19
  383.2 1.3 copy-start.4
  383.5 1.7 copy-start.1
Sparse Core Ops, SparseCore 0:
  58.7 187.8 all-gather.1
where the time goes:
time: 449 us; the launch traced here: 448 us
  waiting for transfers between devices  163 us (36%)
  starting transfers between devices  160 us (36%)
  other arithmetic  55.3 us (12%)
  local copies, waits for them, and re-layouts  40.2 us (9%)
  matrix products  14.6 us (3%)
  between operations  14.5 us (3%)
    ppermute x2, waiting for transfers between devices, from_behind(): lax.ppermute(value, axis, [(source, source + steps) for source in range(f...  109 us
    ppermute x4, starting transfers between devices, extended(): lax.ppermute(lax.slice_in_dim(block, block.shape[dim] - width, None, axis...  99.8 us
    scatter-add x1, other arithmetic, per_device(): crop_terms = jnp.zeros((frames * rows * cols, width), jnp.float32).at[cel...  44.7 us
    all_gather x1, waiting for transfers between devices, per_device(): gathered = lax.all_gather(conv_weight, 'wa', axis=0, tiled=True)  43.4 us
    ppermute x2, starting transfers between devices, from_behind(): lax.ppermute(value, axis, [(source, source + steps) for source in range(f...  21.7 us
    all_to_all x1, starting transfers between devices, per_device(): lax.all_to_all(meta_sent, ('ha', 'wa'), split_axis=0, concat_axis=0, tile...  16.4 us
    all_to_all x1, starting transfers between devices, per_device(): lax.all_to_all(packed, ('ha', 'wa'), split_axis=0, concat_axis=0, tiled=T...  13.4 us
    unnamed x32, local copies, waits for them, and re-layouts  11.2 us
  transfers between devices with their start and end apart: 13, of which 5 were waited for; matrix products, arithmetic and copies ran while one was open for 10% of the time, Pallas kernels for 0%

commit v1 on v0

--- a/solution.py
+++ b/solution.py
@@ -103,7 +103,9 @@
         .at[cell_index.reshape(-1)]
         .add(received.reshape(-1, width).astype(jnp.float32))
     )
-    gathered = lax.all_gather(conv_weight, "wa", axis=0, tiled=True)
+    gathered = jnp.concatenate(
+        lax.all_to_all(jnp.stack([conv_weight] * lax.axis_size("wa")), "wa", 0, 0), axis=0
+    )
     kernel_taps = gathered.reshape(27, width, width)
     past = from_behind(features, "ta", 1)
     padded = widen(jnp.concatenate([past, features], 0))

time: 449 us -> 541 us (1.20)
  waiting for transfers between devices: 163 us -> 222 us
  starting transfers between devices: 160 us -> 191 us
  blocking collectives: 0 us -> 28 us
  between operations: 14.5 us -> 1.21 us
    all_to_all x1, waiting for transfers between devices: 0.01 us -> 119 us  [per_device(): lax.all_to_all(jnp.stack([conv_weight] * lax.axis_size('wa')), 'wa', 0, 0)]
    all_gather x1 -> x0, waiting for transfers between devices: 43.4 us -> none  [per_device(): gathered = lax.all_gather(conv_weight, 'wa', axis=0, tiled=True)]
    ppermute x4, starting transfers between devices: 99.8 us -> 131 us  [extended(): lax.ppermute(lax.slice_in_dim(block, block.shape[dim] - width, None, axis...]
    all_to_all x0 -> x1, blocking collectives: none -> 28 us  [per_device(): lax.all_to_all(meta_sent, ('ha', 'wa'), split_axis=0, concat_axis=0, tile...]
    all_to_all x1, starting transfers between devices: 13.4 us -> 31.5 us  [per_device(): lax.all_to_all(packed, ('ha', 'wa'), split_axis=0, concat_axis=0, tiled=T...]
    ppermute x2, waiting for transfers between devices: 109 us -> 93.7 us  [from_behind(): lax.ppermute(value, axis, [(source, source + steps) for source in range(f...]
    all_to_all x1, starting transfers between devices: 16.4 us -> 4.78 us  [per_device(): lax.all_to_all(jnp.stack([conv_weight] * lax.axis_size('wa')), 'wa', 0, 0)]
    ppermute x2, starting transfers between devices: 21.7 us -> 14.3 us  [from_behind(): lax.ppermute(value, axis, [(source, source + steps) for source in range(f...]
  transfers between devices with their start and end apart: 13 -> 12, of which waited for: 5 -> 6; matrix products, arithmetic and copies ran while one was open for 10% -> 5% of each run, Pallas kernels for 0% -> 0%
where the time goes in v1:
time: 541 us; the launch traced here: 540 us
  waiting for transfers between devices  222 us (41%)
  starting transfers between devices  191 us (35%)
  other arithmetic  51.2 us (9%)
  local copies, waits for them, and re-layouts  37 us (7%)
  blocking collectives  28 us (5%)
  matrix products  9.22 us (2%)
    ppermute x4, starting transfers between devices, extended(): lax.ppermute(lax.slice_in_dim(block, block.shape[dim] - width, None, axis...  131 us
    all_to_all x1, waiting for transfers between devices, per_device(): lax.all_to_all(jnp.stack([conv_weight] * lax.axis_size('wa')), 'wa', 0, 0)  119 us
    ppermute x2, waiting for transfers between devices, from_behind(): lax.ppermute(value, axis, [(source, source + steps) for source in range(f...  93.7 us
    scatter-add x1, other arithmetic, per_device(): crop_terms = jnp.zeros((frames * rows * cols, width), jnp.float32).at[cel...  44.7 us
    all_to_all x1, starting transfers between devices, per_device(): lax.all_to_all(packed, ('ha', 'wa'), split_axis=0, concat_axis=0, tiled=T...  31.5 us
    all_to_all x1, blocking collectives, per_device(): lax.all_to_all(meta_sent, ('ha', 'wa'), split_axis=0, concat_axis=0, tile...  28 us
    ppermute x2, starting transfers between devices, from_behind(): lax.ppermute(value, axis, [(source, source + steps) for source in range(f...  14.3 us
  transfers between devices with their start and end apart: 12, of which 6 were waited for; matrix products, arithmetic and copies ran while one was open for 5% of the time, Pallas kernels for 0%

profile of v1, /device:TPU:27, one launch (start us, length us, event | category | flops | bytes accessed | tf_op | source)
XLA Modules:
  0.0 540.4 jit_solution(17558299741106687546)
XLA Ops:
  4.0 28.0 %all_to_all.26 = s32[64,2,3]{2,1,0:T(2,128)S(1)} all-to-all(s32[64,2,3]{2,1,0:T(2,128)S(1)} %bitcast.92), channel_id=1, replica_groups=mesh['ta'=8,'ha'=4,'wa'=16] {'ha','wa'}, dimensions={0} | all-to-all | bytes 3072 | tf_op jit(solution)/shard_map/all_to_all | solution.py:91
  32.1 2.9 stack.10
  35.0 4.8 all-to-all-start
  41.3 3.4 convolution_convert_fusion
  44.7 7.6 %all_to_all.21 = bf16[64,2,16384]{2,1,0:T(2,128)(2,1)} reshape(bf16[128,16384]{1,0:T(8,128)(2,1)} %convolution_convert_fusion) | data formatting | bytes 8388608 | tf_op jit(solution)/shard_map/all_to_all | solution.py:90
  52.3 119.1 %all-to-all-done = bf16[16,432,256]{2,1,0:T(8,128)(2,1)} async-done(((bf16[16,432,256]{2,1,0:T(8,128)(2,1)}), bf16[16,432,256]{2,1,0:T(8,128)(2,1)}, u32[]{:S(2)}, u32[]{:S(2)}) %all-to-all-start) | async-done | bytes 3538976 | tf_op jit(solution)/shard_map/all_to_all | solution.py:107
  171.3 31.5 %all-to-all-start.2 = ((bf16[64,2,16384]{2,1,0:T(2,128)(2,1)}), bf16[64,2,16384]{2,1,0:T(2,128)(2,1)}, u32[]{:S(2)}, u32[]{:S(2)}) async-start(bf16[64,2,16384]{2,1,0:T(2,128)(2,1)} %all_to_all.21), calls=%async_computation.2 | async-start | bytes 8388608 | tf_op jit(solution)/shard_map/all_to_all | solution.py:90
  202.9 7.9 %collective-permute-start = (bf16[2,16,16,256]{3,2,1,0:T(8,128)(2,1)S(1)}, bf16[2,16,16,256]{3,2,1,0:T(8,128)(2,1)S(1)}, u32[]{:S(2)}, u32[]{:S(2)}) collective-permute-start(bf16[2,16,16,256]{3,2,1,0:T(8,128)(2,1)S(1)} %copy-done.2), channel_id=1, source_target_pairs={{0,64},{64,128},{128,192},{192,256},{256,320},{320,384},{384,448},... | collective-permute-start | bytes 786440 | tf_op jit(solution)/shard_map/ppermute | solution.py:27
  212.0 87.6 %collective-permute-done = bf16[2,16,16,256]{3,2,1,0:T(8,128)(2,1)S(1)} collective-permute-done((bf16[2,16,16,256]{3,2,1,0:T(8,128)(2,1)S(1)}, bf16[2,16,16,256]{3,2,1,0:T(8,128)(2,1)S(1)}, u32[]{:S(2)}, u32[]{:S(2)}) %collective-permute-start) | collective-permute-done | bytes 262176 | tf_op jit(solution)/shard_map/ppermute | solution.py:27
  299.7 3.2 collective-permute-start.1
  305.5 2.5 collective-permute-done.2
  310.1 3.1 collective-permute-start.4
  313.3 3.4 collective-permute-done.4
  318.3 2.2 fusion.23
  323.2 6.3 %collective-permute-start.5 = (bf16[2,16,16,256]{3,2,1,0:T(8,128)(2,1)S(1)}, bf16[2,16,16,256]{3,2,1,0:T(8,128)(2,1)S(1)}, u32[]{:S(2)}, u32[]{:S(2)}) collective-permute-start(bf16[2,16,16,256]{3,2,1,0:T(8,128)(2,1)S(1)} %get-tuple-element.78), channel_id=1, source_target_pairs={{64,0},{128,64},{192,128},{256,192},{320,256},{384,320},{448,384},... | collective-permute-start | bytes 786440 | tf_op jit(solution)/shard_map/ppermute | solution.py:27
  330.0 2.4 reverse_bitcast_fusion
  334.1 6.1 %collective-permute-done.5 = bf16[2,16,16,256]{3,2,1,0:T(8,128)(2,1)S(1)} collective-permute-done((bf16[2,16,16,256]{3,2,1,0:T(8,128)(2,1)S(1)}, bf16[2,16,16,256]{3,2,1,0:T(8,128)(2,1)S(1)}, u32[]{:S(2)}, u32[]{:S(2)}) %collective-permute-start.5) | collective-permute-done | bytes 262176 | tf_op jit(solution)/shard_map/ppermute | solution.py:27
  340.2 2.9 collective-permute-start.6
  343.2 2.4 collective-permute-start.7
  346.4 2.4 copy.76
  352.1 123.2 %collective-permute-start.8 = (bf16[4,18,1,256]{3,2,1,0:T(2,128)(2,1)S(1)}, bf16[4,18,1,256]{3,2,1,0:T(2,128)(2,1)S(1)}, u32[]{:S(2)}, u32[]{:S(2)}) collective-permute-start(bf16[4,18,1,256]{3,2,1,0:T(2,128)(2,1)S(1)} %get-tuple-element.57), channel_id=1, source_target_pairs={{0,1},{1,2},{2,3},{3,4},{4,5},{5,6},{6,7},{7,8},{8,9},{9,10},{10,1... | collective-permute-start | bytes 110600 | tf_op jit(solution)/shard_map/ppermute | solution.py:16
  477.3 3.6 collective-permute-done.9
  485.9 8.2 %reshape.229 = f32[8192,256]{1,0:T(8,128)} reshape(bf16[64,2,16384]{2,1,0:T(2,128)(2,1)} %all-to-all-done.2) | data formatting | bytes 12582912 | tf_op jit(solution)/shard_map/convert_element_type | solution.py:104
  494.1 44.7 %scatter_custom_fusion = f32[512,256]{1,0:T(8,128)S(1)} fusion(s32[8192]{0:T(1024)S(1)} %bitcast.94, f32[8192,256]{1,0:T(8,128)} %reshape.229, f32[]{:T(128)} %constant.7.clone.1), kind=kCustom, calls=%fused_computation.92 | custom fusion | flops 2097152 | bytes 524800 | tf_op jit(solution)/shard_map/scatter-add | solution.py:104
  (90 shorter events, 29.6 us)
Async XLA Ops:
  0.6 210.2 %copy-start = (bf16[2,2,256,256]{3,2,1,0:T(8,128)(2,1)S(1)}, bf16[2,2,256,256]{3,2,1,0:T(8,128)(2,1)}, u32[]{:S(2)}) copy-start(bf16[2,2,256,256]{3,2,1,0:T(8,128)(2,1)} %param.12) | copy-start | bytes 1572868
  35.0 4.8 copy-start.6
  35.0 4.8 copy-start.3
  35.0 136.4 %all-to-all-start = ((bf16[16,432,256]{2,1,0:T(8,128)(2,1)}), bf16[16,432,256]{2,1,0:T(8,128)(2,1)}, u32[]{:S(2)}, u32[]{:S(2)}) async-start(bf16[16,432,256]{2,1,0:T(8,128)(2,1)} %stack.10), calls=%async_computation | async-start | bytes 7077888 | tf_op jit(solution)/shard_map/all_to_all | solution.py:107
  52.3 150.6 %copy-start.2 = (bf16[2,16,16,256]{3,2,1,0:T(8,128)(2,1)S(1)}, bf16[2,16,16,256]{3,2,1,0:T(8,128)(2,1)}, u32[]{:S(2)}) copy-start(bf16[2,16,16,256]{3,2,1,0:T(8,128)(2,1)} %param.10) | copy-start | bytes 786436
  52.3 158.6 %copy-start.5 = (bf16[2,8,8,256]{3,2,1,0:T(8,128)(2,1)S(1)}, bf16[2,8,8,256]{3,2,1,0:T(8,128)(2,1)}, u32[]{:S(2)}) copy-start(bf16[2,8,8,256]{3,2,1,0:T(8,128)(2,1)} %param.13) | copy-start | bytes 196612
  171.3 314.6 %all-to-all-start.2 = ((bf16[64,2,16384]{2,1,0:T(2,128)(2,1)}), bf16[64,2,16384]{2,1,0:T(2,128)(2,1)}, u32[]{:S(2)}, u32[]{:S(2)}) async-start(bf16[64,2,16384]{2,1,0:T(2,128)(2,1)} %all_to_all.21), calls=%async_computation.2 | async-start | bytes 8388608 | tf_op jit(solution)/shard_map/all_to_all | solution.py:90
  202.9 96.8 %collective-permute-start = (bf16[2,16,16,256]{3,2,1,0:T(8,128)(2,1)S(1)}, bf16[2,16,16,256]{3,2,1,0:T(8,128)(2,1)S(1)}, u32[]{:S(2)}, u32[]{:S(2)}) collective-permute-start(bf16[2,16,16,256]{3,2,1,0:T(8,128)(2,1)S(1)} %copy-done.2), channel_id=1, source_target_pairs={{0,64},{64,128},{128,192},{192,256},{256,320},{320,384},{384,448},... | collective-permute-start | bytes 786440 | tf_op jit(solution)/shard_map/ppermute | solution.py:27
  299.7 5.8 %collective-permute-start.1 = (bf16[4,1,16,256]{3,2,1,0:T(8,128)(2,1)S(1)}, bf16[4,1,16,256]{3,2,1,0:T(8,128)(2,1)S(1)}, u32[]{:S(2)}, u32[]{:S(2)}) collective-permute-start(bf16[4,1,16,256]{3,2,1,0:T(8,128)(2,1)S(1)} %get-tuple-element.80), channel_id=1, source_target_pairs={{0,16},{16,32},{32,48},{1,17},{17,33},{33,49},{2,18},{18,34},{34,5... | collective-permute-start | bytes 98312 | tf_op jit(solution)/shard_map/ppermute | solution.py:16
  302.9 5.1 collective-permute-start.2
  308.1 5.1 collective-permute-start.3
  310.1 6.6 %collective-permute-start.4 = (bf16[4,18,1,256]{3,2,1,0:T(2,128)(2,1)S(1)}, bf16[4,18,1,256]{3,2,1,0:T(2,128)(2,1)S(1)}, u32[]{:S(2)}, u32[]{:S(2)}) collective-permute-start(bf16[4,18,1,256]{3,2,1,0:T(2,128)(2,1)S(1)} %get-tuple-element.60), channel_id=1, source_target_pairs={{1,0},{2,1},{3,2},{4,3},{5,4},{6,5},{7,6},{8,7},{9,8},{10,9},{11,1... | collective-permute-start | bytes 110600 | tf_op jit(solution)/shard_map/ppermute | solution.py:19
  323.2 17.1 %collective-permute-start.5 = (bf16[2,16,16,256]{3,2,1,0:T(8,128)(2,1)S(1)}, bf16[2,16,16,256]{3,2,1,0:T(8,128)(2,1)S(1)}, u32[]{:S(2)}, u32[]{:S(2)}) collective-permute-start(bf16[2,16,16,256]{3,2,1,0:T(8,128)(2,1)S(1)} %get-tuple-element.78), channel_id=1, source_target_pairs={{64,0},{128,64},{192,128},{256,192},{320,256},{384,320},{448,384},... | collective-permute-start | bytes 786440 | tf_op jit(solution)/shard_map/ppermute | solution.py:27
  340.2 11.7 %collective-permute-start.6 = (bf16[4,1,16,256]{3,2,1,0:T(8,128)(2,1)S(1)}, bf16[4,1,16,256]{3,2,1,0:T(8,128)(2,1)S(1)}, u32[]{:S(2)}, u32[]{:S(2)}) collective-permute-start(bf16[4,1,16,256]{3,2,1,0:T(8,128)(2,1)S(1)} %get-tuple-element.76), channel_id=1, source_target_pairs={{0,16},{16,32},{32,48},{1,17},{17,33},{33,49},{2,18},{18,34},{34,5... | collective-permute-start | bytes 98312 | tf_op jit(solution)/shard_map/ppermute | solution.py:16
  343.2 8.8 %collective-permute-start.7 = (bf16[4,1,16,256]{3,2,1,0:T(8,128)(2,1)S(1)}, bf16[4,1,16,256]{3,2,1,0:T(8,128)(2,1)S(1)}, u32[]{:S(2)}, u32[]{:S(2)}) collective-permute-start(bf16[4,1,16,256]{3,2,1,0:T(8,128)(2,1)S(1)} %get-tuple-element.77), channel_id=1, source_target_pairs={{16,0},{32,16},{48,32},{17,1},{33,17},{49,33},{18,2},{34,18},{50,3... | collective-permute-start | bytes 98312 | tf_op jit(solution)/shard_map/ppermute | solution.py:19
  352.1 125.3 %collective-permute-start.8 = (bf16[4,18,1,256]{3,2,1,0:T(2,128)(2,1)S(1)}, bf16[4,18,1,256]{3,2,1,0:T(2,128)(2,1)S(1)}, u32[]{:S(2)}, u32[]{:S(2)}) collective-permute-start(bf16[4,18,1,256]{3,2,1,0:T(2,128)(2,1)S(1)} %get-tuple-element.57), channel_id=1, source_target_pairs={{0,1},{1,2},{2,3},{3,4},{4,5},{5,6},{6,7},{7,8},{8,9},{9,10},{10,1... | collective-permute-start | bytes 110600 | tf_op jit(solution)/shard_map/ppermute | solution.py:16
  475.3 5.7 %collective-permute-start.9 = (bf16[4,18,1,256]{3,2,1,0:T(2,128)(2,1)S(1)}, bf16[4,18,1,256]{3,2,1,0:T(2,128)(2,1)S(1)}, u32[]{:S(2)}, u32[]{:S(2)}) collective-permute-start(bf16[4,18,1,256]{3,2,1,0:T(2,128)(2,1)S(1)} %get-tuple-element.56), channel_id=1, source_target_pairs={{1,0},{2,1},{3,2},{4,3},{5,4},{6,5},{7,6},{8,7},{9,8},{10,9},{11,1... | collective-permute-start | bytes 110600 | tf_op jit(solution)/shard_map/ppermute | solution.py:19
  482.3 1.3 copy-start.4
  482.6 1.7 copy-start.1
